TPU v7x, 32 devices: a whole 2x2x4 slice. The times are simulated.
32 devices in a mesh: group: 4 (over y, x), member: 8 (over z, core).
Axes of the slice: x: 2, y: 2, z: 4, core: 2. Of those that a mesh axis runs over, the one named last changes fastest.
Arguments:
- activations: bfloat16 [4, 1024, 2048], P('group', 'member'), may hold values from -6 to 6
- lengths: int32 [4, 8], P('group'), may hold values from 1 to 128, 576 in all within a row
- assignment: int32 [4, 8], P('group'), may hold values from 0 to 7, each once within a row
- owners: int32 [4], replicated, may hold values from 0 to 3
- prefix_cache: bfloat16 [4, 8192, 256], P('group', 'member'), may hold values from -244 to 244
- first_gain: float32 [2048], replicated, may hold values from 0.1 to 1.9
- first_bias: float32 [2048], replicated, may hold values from -3 to 3
- query_weight: bfloat16 [2048, 2048], replicated, may hold values from -0.125 to 0.125
- keyval_weight: bfloat16 [2048, 256], replicated, may hold values from -0.4375 to 0.4375
- output_weight: bfloat16 [2048, 2048], replicated, may hold values from -0.125 to 0.125
- second_gain: float32 [2048], replicated, may hold values from 0.1 to 1.9
- second_bias: float32 [2048], replicated, may hold values from -3 to 3
- expand_weight: bfloat16 [2048, 8192], P(None, 'member'), may hold values from -0.125 to 0.125
- contract_weight: bfloat16 [8192, 2048], P('member'), may hold values from -0.0625 to 0.0625
Outputs:
- layer_output: bfloat16 [4, 1024, 2048], P('group', 'member')
Inputs may be any that keep to these rules, and one draw needn't show every extreme that they name: Each row of lengths sums to 576 and its longest entry is 128. Each row of assignment names every request of its group once. `owners`: several groups may attend the same cache slot.
All inputs are finite; a program needn't handle non-finite values.
Results may differ from a plain program's by a relative error of at most 0.011.
The roundings to bfloat16 on the way count: a program that leaves them out, or rounds other values in their place, can miss the bound.
Values may be sent and summed in bfloat16 or wider, within the bound.
No kernel may reach another device: no remote copies, remote signals or barrier semaphores. Data moves between devices by JAX's collectives and lax.ppermute only.
A program may use at most 128 MiB of HBM per device.

v0:
```python
import math
import jax
import jax.numpy as jnp
from jax import lax
from jax.sharding import PartitionSpec as P

EPSILON = 1e-05
NEGATIVE = -1e30


def layer_norm(values, gain, bias):
    average = jnp.mean(values, axis=-1, keepdims=True)
    centered = values - average
    spread = jnp.mean(centered * centered, axis=-1, keepdims=True)
    return centered * lax.rsqrt(spread + EPSILON) * gain + bias


def pick_value(table, wanted):
    slots_at = lax.broadcasted_iota(jnp.int32, table.shape, 0)
    return jnp.sum(jnp.where(slots_at == wanted, table, 0))


def own_scores(query_block, own_keys, scaling):
    scores = (
        jnp.einsum("thd,sd->ths", query_block, own_keys, preferred_element_type=jnp.float32)
        * scaling
    )
    block_rows = query_block.shape[0]
    key_rows = own_keys.shape[0]
    row_at = lax.broadcasted_iota(jnp.int32, (block_rows, 1, key_rows), 0)
    column_at = lax.broadcasted_iota(jnp.int32, (block_rows, 1, key_rows), 2)
    return jnp.where(column_at <= row_at, scores, NEGATIVE)


def folded_attention(queries, keys_values, selected):
    row_count, head_count, head_size = queries.shape
    scaling = 1.0 / math.sqrt(head_size)
    own_keys = keys_values[:, :head_size]
    own_values = keys_values[:, head_size:]
    suffix_scores = own_scores(queries, own_keys, scaling)
    highest = jnp.max(suffix_scores, axis=-1)
    suffix_exp = jnp.exp(suffix_scores - highest[..., None])
    denominator = jnp.sum(suffix_exp, axis=-1)
    weighted = jnp.einsum(
        "ths,sd->thd",
        suffix_exp.astype(jnp.bfloat16),
        own_values,
        preferred_element_type=jnp.float32,
    )
    running = (weighted, highest, denominator)
    portion = lax.all_gather(selected, "member", axis=0, tiled=True)
    extent = portion.shape[0]
    stride = math.gcd(extent, 1024)

    def advance(state_now, block_index):
        weighted_now, highest_now, denominator_now = state_now
        key_block = lax.dynamic_slice_in_dim(portion, block_index * stride, stride, 0)
        scores = (
            jnp.einsum(
                "thd,pd->thp", queries, key_block[:, :head_size], preferred_element_type=jnp.float32
            )
            * scaling
        )
        highest_next = jnp.maximum(highest_now, jnp.max(scores, axis=-1))
        rescale = jnp.exp(highest_now - highest_next)
        exponent = jnp.exp(scores - highest_next[..., None])
        denominator_next = denominator_now * rescale + jnp.sum(exponent, axis=-1)
        weighted_next = weighted_now * rescale[..., None] + jnp.einsum(
            "thp,pd->thd",
            exponent.astype(jnp.bfloat16),
            key_block[:, head_size:],
            preferred_element_type=jnp.float32,
        )
        return ((weighted_next, highest_next, denominator_next), None)

    running, _ = lax.scan(advance, running, jnp.arange(extent // stride, dtype=jnp.int32))
    weighted, highest, denominator = running
    return (
        (weighted / denominator[..., None])
        .astype(jnp.bfloat16)
        .reshape(row_count, head_count * head_size)
    )


def shards(
    activations,
    lengths,
    assignment,
    owners,
    prefix_cache,
    first_gain,
    first_bias,
    query_weight,
    keyval_weight,
    output_weight,
    second_gain,
    second_bias,
    expand_weight,
    contract_weight,
):
    group_index = lax.axis_index("group")
    member_index = lax.axis_index("member")
    request = pick_value(assignment[0], member_index)
    length_here = pick_value(lengths[0], request)
    owner_here = pick_value(owners, group_index)
    tokens = activations[0]
    row_count = tokens.shape[0]
    head_size = prefix_cache.shape[2] // 2
    head_count = tokens.shape[1] // head_size
    every_block = lax.all_gather(prefix_cache, "group", axis=0, tiled=True)
    selected = lax.dynamic_index_in_dim(every_block, owner_here, 0, keepdims=False)
    tokens_wide = tokens.astype(jnp.float32)
    normed = layer_norm(tokens_wide, first_gain, first_bias).astype(jnp.bfloat16)
    queries = jnp.dot(normed, query_weight, preferred_element_type=jnp.float32).astype(jnp.bfloat16)
    queries = queries.reshape(row_count, head_count, head_size)
    keys_values = jnp.dot(normed, keyval_weight, preferred_element_type=jnp.float32).astype(
        jnp.bfloat16
    )
    attended = folded_attention(queries, keys_values, selected)
    residual = tokens_wide + jnp.dot(attended, output_weight, preferred_element_type=jnp.float32)
    second = layer_norm(residual, second_gain, second_bias).astype(jnp.bfloat16)
    hidden = jax.nn.gelu(
        jnp.dot(
            lax.all_gather(second, "member", axis=0, tiled=True),
            expand_weight,
            preferred_element_type=jnp.float32,
        ),
        approximate=True,
    ).astype(jnp.bfloat16)
    summed = lax.psum_scatter(
        jnp.dot(hidden, contract_weight, preferred_element_type=jnp.float32).astype(jnp.bfloat16),
        "member",
        scatter_dimension=0,
        tiled=True,
    ).astype(jnp.float32)
    is_live = lax.broadcasted_iota(jnp.int32, (row_count, 1), 0) < length_here
    return jnp.where(is_live, residual + summed, 0.0).astype(jnp.bfloat16)[None]


def solution(mesh):
    return jax.shard_map(
        shards,
        mesh=mesh,
        in_specs=(
            P("group", "member", None),
            P("group", None),
            P("group", None),
            P(),
            P("group", "member", None),
            P(),
            P(),
            P(),
            P(),
            P(),
            P(),
            P(),
            P(None, "member"),
            P("member", None),
        ),
        out_specs=P("group", "member", None),
        check_vma=False,
    )
```

profile of v0, /device:TPU:0, one launch (start us, length us, event | category | flops | bytes accessed | tf_op | source)
XLA Modules:
  0.0 286.6 jit_solution(2638500522030421383)
XLA Ops:
  10.5 36.7 %all-gather.5.cloned.1.call-done = bf16[4,1024,256]{2,1,0:T(8,128)(2,1)} async-done(((bf16[1,1024,256]{2,1,0:T(8,128)(2,1)}), bf16[4,1024,256]{2,1,0:T(8,128)(2,1)}) %all-gather.5.cloned.1.call-update) | async-done | bytes 2097168 | tf_op jit(solution)/shard_map/all_gather | solution.py:110
  47.2 1.9 constant_dynamic-slice_fusion
  51.8 5.0 %fusion.30 = bf16[16,16,8,128]{3,2,1,0:T(8,128)(2,1)S(1)} fusion(bf16[2048,2048]{1,0:T(8,128)(2,1)} %param.23, bf16[1,128,2048]{2,1,0:T(8,128)(2,1)} %param.16, f32[2048]{0:T(1024)} %param.22, f32[2048]{0:T(1024)} %param.21, f32[128]{0:T(128)S(1)} %add_rsqrt_fusion.1, f32[128]{0:T(128)S(1)} %broadcast_multiply_fusion.1), kind=kOutput, calls=%fused_computation.39 | convolution fusion | flops 1075576832 | bytes 9454592 | tf_op jit(solution)/shard_map/dot_general | solution.py:114
  58.2 38.3 %all-gather.9.cloned.1.call-done = bf16[1,8192,256]{2,1,0:T(8,128)(2,1)} async-done(((bf16[1,1024,256]{2,1,0:T(8,128)(2,1)}), bf16[1,8192,256]{2,1,0:T(8,128)(2,1)}) %all-gather.9.cloned.1.call-update) | async-done | bytes 4194320 | tf_op jit(solution)/shard_map/all_gather | solution.py:51
  96.4 62.7 %while.14 = (s32[]{:T(128)}, f32[128,16,128]{2,0,1:T(8,128)S(1)}, f32[128,16]{0,1:T(8,128)S(1)}, f32[128,16]{0,1:T(8,128)S(1)}, s32[8]{0:T(128)S(1)}, /*index=5*...) while((s32[]{:T(128)}, f32[128,16,128]{2,0,1:T(8,128)S(1)}, ...), condition=%wide.region_10.11_spmd, body=%wide.region_7.10_spmd.sunk | while | flops 1091047424 | bytes 28442832 | solution.py:76
  97.7 2.2 bitcast_reduce_fusion.2
  99.9 1.4 fusion.68
  101.3 2.9 %fusion.69 = f32[128,16,128]{2,0,1:T(8,128)S(1)} fusion(f32[1024,128,16]{1,0,2:T(8,128)S(1)} %get-tuple-element.135, f32[128,16]{0,1:T(8,128)S(1)} %max.4, f32[128,16,128]{2,0,1:T(8,128)S(1)} %get-tuple-element.152, f32[128,16]{0,1:T(8,128)S(1)} %get-tuple-element.137, bf16[8192,256]{1,0:T(8,128)(2,1)} %get-tuple-element.168, s32[]{:T(128)S(6)} %select_n.46, ...), kind=kOutput, calls=%fused_computation.8.clone.1 | convolution fusion | flops 543686656 | bytes 10764296 | tf_op jit(solution)/shard_map/while/body/eval_jaxpr/thp,pd->thd/dot_general | solution.py:68
  105.5 2.2 bitcast_reduce_fusion.2
  107.8 1.4 fusion.68
  109.2 2.9 %fusion.69 = f32[128,16,128]{2,0,1:T(8,128)S(1)} fusion(f32[1024,128,16]{1,0,2:T(8,128)S(1)} %get-tuple-element.135, f32[128,16]{0,1:T(8,128)S(1)} %max.4, f32[128,16,128]{2,0,1:T(8,128)S(1)} %get-tuple-element.152, f32[128,16]{0,1:T(8,128)S(1)} %get-tuple-element.137, bf16[8192,256]{1,0:T(8,128)(2,1)} %get-tuple-element.168, s32[]{:T(128)S(6)} %select_n.46, ...), kind=kOutput, calls=%fused_computation.8.clone.1 | convolution fusion | flops 543686656 | bytes 10764296 | tf_op jit(solution)/shard_map/while/body/eval_jaxpr/thp,pd->thd/dot_general | solution.py:68
  113.4 2.2 bitcast_reduce_fusion.2
  115.6 1.4 fusion.68
  117.0 2.9 %fusion.69 = f32[128,16,128]{2,0,1:T(8,128)S(1)} fusion(f32[1024,128,16]{1,0,2:T(8,128)S(1)} %get-tuple-element.135, f32[128,16]{0,1:T(8,128)S(1)} %max.4, f32[128,16,128]{2,0,1:T(8,128)S(1)} %get-tuple-element.152, f32[128,16]{0,1:T(8,128)S(1)} %get-tuple-element.137, bf16[8192,256]{1,0:T(8,128)(2,1)} %get-tuple-element.168, s32[]{:T(128)S(6)} %select_n.46, ...), kind=kOutput, calls=%fused_computation.8.clone.1 | convolution fusion | flops 543686656 | bytes 10764296 | tf_op jit(solution)/shard_map/while/body/eval_jaxpr/thp,pd->thd/dot_general | solution.py:68
  121.2 2.2 bitcast_reduce_fusion.2
  123.4 1.4 fusion.68
  124.8 2.9 %fusion.69 = f32[128,16,128]{2,0,1:T(8,128)S(1)} fusion(f32[1024,128,16]{1,0,2:T(8,128)S(1)} %get-tuple-element.135, f32[128,16]{0,1:T(8,128)S(1)} %max.4, f32[128,16,128]{2,0,1:T(8,128)S(1)} %get-tuple-element.152, f32[128,16]{0,1:T(8,128)S(1)} %get-tuple-element.137, bf16[8192,256]{1,0:T(8,128)(2,1)} %get-tuple-element.168, s32[]{:T(128)S(6)} %select_n.46, ...), kind=kOutput, calls=%fused_computation.8.clone.1 | convolution fusion | flops 543686656 | bytes 10764296 | tf_op jit(solution)/shard_map/while/body/eval_jaxpr/thp,pd->thd/dot_general | solution.py:68
  129.0 2.2 bitcast_reduce_fusion.2
  131.3 1.4 fusion.68
  132.7 2.9 %fusion.69 = f32[128,16,128]{2,0,1:T(8,128)S(1)} fusion(f32[1024,128,16]{1,0,2:T(8,128)S(1)} %get-tuple-element.135, f32[128,16]{0,1:T(8,128)S(1)} %max.4, f32[128,16,128]{2,0,1:T(8,128)S(1)} %get-tuple-element.152, f32[128,16]{0,1:T(8,128)S(1)} %get-tuple-element.137, bf16[8192,256]{1,0:T(8,128)(2,1)} %get-tuple-element.168, s32[]{:T(128)S(6)} %select_n.46, ...), kind=kOutput, calls=%fused_computation.8.clone.1 | convolution fusion | flops 543686656 | bytes 10764296 | tf_op jit(solution)/shard_map/while/body/eval_jaxpr/thp,pd->thd/dot_general | solution.py:68
  136.9 2.2 bitcast_reduce_fusion.2
  139.1 1.4 fusion.68
  140.5 2.9 %fusion.69 = f32[128,16,128]{2,0,1:T(8,128)S(1)} fusion(f32[1024,128,16]{1,0,2:T(8,128)S(1)} %get-tuple-element.135, f32[128,16]{0,1:T(8,128)S(1)} %max.4, f32[128,16,128]{2,0,1:T(8,128)S(1)} %get-tuple-element.152, f32[128,16]{0,1:T(8,128)S(1)} %get-tuple-element.137, bf16[8192,256]{1,0:T(8,128)(2,1)} %get-tuple-element.168, s32[]{:T(128)S(6)} %select_n.46, ...), kind=kOutput, calls=%fused_computation.8.clone.1 | convolution fusion | flops 543686656 | bytes 10764296 | tf_op jit(solution)/shard_map/while/body/eval_jaxpr/thp,pd->thd/dot_general | solution.py:68
  144.7 2.2 bitcast_reduce_fusion.2
  148.4 2.9 %fusion.69 = f32[128,16,128]{2,0,1:T(8,128)S(1)} fusion(f32[1024,128,16]{1,0,2:T(8,128)S(1)} %get-tuple-element.135, f32[128,16]{0,1:T(8,128)S(1)} %max.4, f32[128,16,128]{2,0,1:T(8,128)S(1)} %get-tuple-element.152, f32[128,16]{0,1:T(8,128)S(1)} %get-tuple-element.137, bf16[8192,256]{1,0:T(8,128)(2,1)} %get-tuple-element.168, s32[]{:T(128)S(6)} %select_n.46, ...), kind=kOutput, calls=%fused_computation.8.clone.1 | convolution fusion | flops 543686656 | bytes 10764296 | tf_op jit(solution)/shard_map/while/body/eval_jaxpr/thp,pd->thd/dot_general | solution.py:68
  152.6 2.2 bitcast_reduce_fusion.2
  156.2 2.9 %fusion.69 = f32[128,16,128]{2,0,1:T(8,128)S(1)} fusion(f32[1024,128,16]{1,0,2:T(8,128)S(1)} %get-tuple-element.135, f32[128,16]{0,1:T(8,128)S(1)} %max.4, f32[128,16,128]{2,0,1:T(8,128)S(1)} %get-tuple-element.152, f32[128,16]{0,1:T(8,128)S(1)} %get-tuple-element.137, bf16[8192,256]{1,0:T(8,128)(2,1)} %get-tuple-element.168, s32[]{:T(128)S(6)} %select_n.46, ...), kind=kOutput, calls=%fused_computation.8.clone.1 | convolution fusion | flops 543686656 | bytes 10764296 | tf_op jit(solution)/shard_map/while/body/eval_jaxpr/thp,pd->thd/dot_general | solution.py:68
  161.9 4.8 %fusion.51 = (f32[128]{0:T(128)S(1)}, f32[128,2048]{1,0:T(8,128)S(1)}) fusion(bf16[128,2048]{0,1:T(8,128)(2,1)S(1)} %bitcast.88, bf16[2048,2048]{1,0:T(8,128)(2,1)} %param.25, bf16[1,128,2048]{2,1,0:T(8,128)(2,1)S(1)} %copy-done.1), kind=kOutput, calls=%fused_computation.76 | convolution fusion | flops 1074528128 | bytes 10486272 | tf_op jit(solution)/shard_map/dot_general | solution.py:120
  168.2 45.8 %all-gather.7.cloned.1.call-done = bf16[1024,2048]{1,0:T(8,128)(2,1)} async-done(((bf16[128,2048]{1,0:T(8,128)(2,1)}), bf16[1024,2048]{1,0:T(8,128)(2,1)}) %all-gather.7.cloned.1.call-update) | async-done | bytes 4194320 | tf_op jit(solution)/shard_map/all_gather | solution.py:124
  214.0 15.1 %convolution_convert_fusion = bf16[1024,2048]{1,0:T(8,128)(2,1)} fusion(bf16[1024,2048]{1,0:T(8,128)(2,1)} %param.29, bf16[1024,2048]{1,0:T(8,128)(2,1)} %all-gather.7.cloned.1.call-done, bf16[2048,1024]{1,0:T(8,128)(2,1)} %param.28), kind=kOutput, calls=%fused_computation.25 | convolution fusion | flops 8601468928 | bytes 16777216 | tf_op jit(solution)/shard_map/dot_general | solution.py:131
  232.2 45.8 %reduce-scatter.2.cloned.1.call-done = bf16[128,2048]{1,0:T(8,128)(2,1)} async-done(((bf16[1024,2048]{1,0:T(8,128)(2,1)}), bf16[128,2048]{1,0:T(8,128)(2,1)}) %reduce-scatter.2.cloned.1.call-update) | async-done | bytes 524304 | tf_op jit(solution)/shard_map/reduce_scatter | solution.py:130
  278.0 2.0 fusion.39
  (79 shorter events, 20.9 us)
Async XLA Ops:
  6.5 50.4 %copy-start = (bf16[2048,256]{1,0:T(8,128)(2,1)S(1)}, bf16[2048,256]{1,0:T(8,128)(2,1)}, u32[]{:S(2)}) copy-start(bf16[2048,256]{1,0:T(8,128)(2,1)} %param.24) | copy-start | bytes 3145732
  6.5 40.7 %all-gather.5.cloned.1.call-start = ((), (), s32[]{:S(2)}) async-start(), calls=%async_computation.1 | async-start | bytes 2621440 | tf_op jit(solution)/shard_map/all_gather | solution.py:110
  7.3 89.2 %all-gather.9.cloned.1.call-start = ((), (), s32[]{:S(2)}) async-start(), calls=%async_computation.4 | async-start | bytes 4718592 | tf_op jit(solution)/shard_map/all_gather | solution.py:51
  49.1 164.9 %all-gather.7.cloned.1.call-start = ((), (), s32[]{:S(2)}) async-start(), calls=%async_computation.2 | async-start | bytes 4718592 | tf_op jit(solution)/shard_map/all_gather | solution.py:124
  51.7 5.2 %copy-start.1 = (bf16[1,128,2048]{2,1,0:T(8,128)(2,1)S(1)}, bf16[1,128,2048]{2,1,0:T(8,128)(2,1)}, u32[]{:S(2)}) copy-start(bf16[1,128,2048]{2,1,0:T(8,128)(2,1)} %param.16) | copy-start | bytes 1572868
  51.7 5.2 %copy-start.4 = (f32[2048]{0:T(1024)S(1)}, f32[2048]{0:T(1024)}, u32[]{:S(2)}) copy-start(f32[2048]{0:T(1024)} %param.22) | copy-start | bytes 24580
  51.8 5.2 %copy-start.5 = (f32[2048]{0:T(1024)S(1)}, f32[2048]{0:T(1024)}, u32[]{:S(2)}) copy-start(f32[2048]{0:T(1024)} %param.21) | copy-start | bytes 24580
  161.8 5.1 %copy-start.2 = (f32[2048]{0:T(1024)S(1)}, f32[2048]{0:T(1024)}, u32[]{:S(2)}) copy-start(f32[2048]{0:T(1024)} %param.27) | copy-start | bytes 24580
  161.9 5.1 %copy-start.3 = (f32[2048]{0:T(1024)S(1)}, f32[2048]{0:T(1024)}, u32[]{:S(2)}) copy-start(f32[2048]{0:T(1024)} %param.26) | copy-start | bytes 24580
  168.0 110.1 %reduce-scatter.2.cloned.1.call-start = ((), (), s32[]{:S(2)}) async-start(), calls=%async_computation.3 | async-start | bytes 4718592 | tf_op jit(solution)/shard_map/reduce_scatter | solution.py:130
  229.1 0.7 copy-start.6
  229.1 1.3 copy-start.7
Sparse Core Ops, SparseCore 0:
  9.2 38.0 all-gather.4
  49.3 47.1 all-gather.8
  168.1 45.8 all-gather.6
  229.3 48.7 reduce-scatter.1
where the time goes:
time: 288 us; the launch traced here: 287 us
  waiting for transfers between devices  167 us (58%)
  matrix products  67.1 us (23%)
  other arithmetic  22.2 us (8%)
  between operations  15.2 us (5%)
  local copies, waits for them, and re-layouts  8.7 us (3%)
  loops' own time  5.68 us (2%)
    reduce_scatter x1, waiting for transfers between devices, shards(): lax.psum_scatter(jnp.dot(hidden, contract_weight, preferred_element_type=...  45.8 us
    all_gather x1, waiting for transfers between devices, shards(): lax.all_gather(second, 'member', axis=0, tiled=True)  45.8 us
    all_gather x1, waiting for transfers between devices, folded_attention(): portion = lax.all_gather(selected, 'member', axis=0, tiled=True)  38.3 us
    all_gather x1, waiting for transfers between devices, shards(): every_block = lax.all_gather(prefix_cache, 'group', axis=0, tiled=True)  36.7 us
    dot_general x8, matrix products, advance(): jnp.einsum('thp,pd->thd', exponent.astype(jnp.bfloat16), key_block[:, hea...  23.5 us
    dot_general x8, matrix products, advance(): jnp.einsum('thd,pd->thp', queries, key_block[:, :head_size], preferred_el...  17.7 us
    dot_general x1, matrix products, shards(): jnp.dot(hidden, contract_weight, preferred_element_type=jnp.float32)  15.1 us
    reduce_sum x8, other arithmetic, advance(): denominator_next = denominator_now * rescale + jnp.sum(exponent, axis=-1)  11 us
  transfers between devices with their start and end apart: 4, of which 4 were waited for; matrix products, arithmetic and copies ran while one was open for 4% of the time, Pallas kernels for 0%

commit v1 on v0

--- a/solution.py
+++ b/solution.py
@@ -48,7 +48,24 @@
         preferred_element_type=jnp.float32,
     )
     running = (weighted, highest, denominator)
-    portion = lax.all_gather(selected, "member", axis=0, tiled=True)
+    size, index, width = (lax.axis_size("member"), lax.axis_index("member"), selected.shape[0])
+    upward = [(i, (i + 1) % size) for i in range(size)]
+    backward = [(i, (i - 1) % size) for i in range(size)]
+    whole = jnp.zeros((*selected.shape[:0], size * width, *selected.shape[0 + 1 :]), selected.dtype)
+    whole = lax.dynamic_update_slice_in_dim(whole, selected, index * width, axis=0)
+    from_left = from_right = selected
+    half = size // 2
+    for turn in range(1, half + 1):
+        from_left = lax.ppermute(from_left, "member", upward)
+        whole = lax.dynamic_update_slice_in_dim(
+            whole, from_left, (index - turn) % size * width, axis=0
+        )
+        if turn < size - half:
+            from_right = lax.ppermute(from_right, "member", backward)
+            whole = lax.dynamic_update_slice_in_dim(
+                whole, from_right, (index + turn) % size * width, axis=0
+            )
+    portion = whole
     extent = portion.shape[0]
     stride = math.gcd(extent, 1024)
 

time: 288 us -> 295 us (1.024)
  waiting for transfers between devices: 167 us -> 152 us
  local copies, waits for them, and re-layouts: 8.7 us -> 19.6 us
  starting transfers between devices: 0.31 us -> 11.1 us
    all_gather x1 -> x0, waiting for transfers between devices: 38.3 us -> none  [folded_attention(): portion = lax.all_gather(selected, 'member', axis=0, tiled=True)]
    ppermute x0 -> x7, waiting for transfers between devices: none -> 26.9 us  [the longest x4 26.9 us: folded_attention(): from_left = lax.ppermute(from_left, 'member', upward)]
    dynamic_update_slice x0 -> x8, local copies, waits for them, and re-layouts: none -> 11.2 us  [the longest x4 5.43 us: folded_attention(): lax.dynamic_update_slice_in_dim(whole, from_left, (index - turn) % size *...]
    ppermute x0 -> x7, starting transfers between devices: none -> 10.8 us  [the longest x3 10.7 us: folded_attention(): from_right = lax.ppermute(from_right, 'member', backward)]
  transfers between devices with their start and end apart: 4 -> 10, of which waited for: 4 -> 7; matrix products, arithmetic and copies ran while one was open for 4% -> 8% of each run, Pallas kernels for 0% -> 0%
where the time goes in v1:
time: 295 us; the launch traced here: 294 us
  waiting for transfers between devices  152 us (52%)
  matrix products  68.1 us (23%)
  other arithmetic  22.2 us (8%)
  local copies, waits for them, and re-layouts  19.6 us (7%)
  between operations  15.4 us (5%)
  starting transfers between devices  11.1 us (4%)
  loops' own time  5.68 us (2%)
    reduce_scatter x1, waiting for transfers between devices, shards(): lax.psum_scatter(jnp.dot(hidden, contract_weight, preferred_element_type=...  45.8 us
    all_gather x1, waiting for transfers between devices, shards(): lax.all_gather(second, 'member', axis=0, tiled=True)  44.3 us
    all_gather x1, waiting for transfers between devices, shards(): every_block = lax.all_gather(prefix_cache, 'group', axis=0, tiled=True)  34.2 us
    ppermute x4, waiting for transfers between devices, folded_attention(): from_left = lax.ppermute(from_left, 'member', upward)  26.9 us
    dot_general x8, matrix products, advance(): jnp.einsum('thp,pd->thd', exponent.astype(jnp.bfloat16), key_block[:, hea...  23.5 us
    dot_general x8, matrix products, advance(): jnp.einsum('thd,pd->thp', queries, key_block[:, :head_size], preferred_el...  17.7 us
    dot_general x1, matrix products, shards(): jnp.dot(hidden, contract_weight, preferred_element_type=jnp.float32)  15.1 us
    reduce_sum x8, other arithmetic, advance(): denominator_next = denominator_now * rescale + jnp.sum(exponent, axis=-1)  11 us
  transfers between devices with their start and end apart: 10, of which 7 were waited for; matrix products, arithmetic and copies ran while one was open for 8% of the time, Pallas kernels for 0%

profile of v1, /device:TPU:0, one launch (start us, length us, event | category | flops | bytes accessed | tf_op | source)
XLA Modules:
  0.0 293.9 jit_solution(3526777746959075713)
XLA Ops:
  13.1 34.2 %all-gather.3.cloned.1.call-done = bf16[4,1024,256]{2,1,0:T(8,128)(2,1)} async-done(((bf16[1,1024,256]{2,1,0:T(8,128)(2,1)}), bf16[4,1024,256]{2,1,0:T(8,128)(2,1)}) %all-gather.3.cloned.1.call-update) | async-done | bytes 2097168 | tf_op jit(solution)/shard_map/all_gather | solution.py:127
  48.7 3.5 %collective-permute-start.1 = (bf16[1024,256]{1,0:T(8,128)(2,1)S(1)}, bf16[1024,256]{1,0:T(8,128)(2,1)}, u32[]{:S(2)}, u32[]{:S(2)}) collective-permute-start(bf16[1024,256]{1,0:T(8,128)(2,1)S(1)} %get-tuple-element.83), channel_id=1, source_target_pairs={{0,7},{1,0},{2,1},{3,2},{4,3},{5,4},{6,5},{7,6},{8,15},{9,8},{10,9... | collective-permute-start | bytes 1572872 | tf_op jit(solution)/shard_map/ppermute | solution.py:64
  52.3 4.7 %fusion.30 = bf16[16,16,8,128]{3,2,1,0:T(8,128)(2,1)S(1)} fusion(bf16[2048,2048]{1,0:T(8,128)(2,1)} %param.23, bf16[1,128,2048]{2,1,0:T(8,128)(2,1)S(1)} %copy-done.2, f32[2048]{0:T(1024)S(1)} %copy-done.7, f32[2048]{0:T(1024)S(1)} %copy-done.8, f32[128]{0:T(128)S(1)} %add_rsqrt_fusion.1, f32[128]{0:T(128)S(1)} %broadcast_multiply_fusion.1), kind=kOutput, calls=%fused_computation.39 | convolution fusion | flops 1075576832 | bytes 9454592 | tf_op jit(solution)/shard_map/dot_general | solution.py:131
  57.1 5.9 %collective-permute-done = bf16[1024,256]{1,0:T(8,128)(2,1)} collective-permute-done((bf16[1024,256]{1,0:T(8,128)(2,1)S(1)}, bf16[1024,256]{1,0:T(8,128)(2,1)}, u32[]{:S(2)}, u32[]{:S(2)}) %collective-permute-start) | collective-permute-done | bytes 524320 | tf_op jit(solution)/shard_map/ppermute | solution.py:59
  63.4 3.6 %collective-permute-start.3 = (bf16[1024,256]{1,0:T(8,128)(2,1)}, bf16[1024,256]{1,0:T(8,128)(2,1)}, u32[]{:S(2)}, u32[]{:S(2)}) collective-permute-start(bf16[1024,256]{1,0:T(8,128)(2,1)} %collective-permute-done.1), channel_id=1, source_target_pairs={{0,7},{1,0},{2,1},{3,2},{4,3},{5,4},{6,5},{7,6},{8,15},{9,8},{10,9... | collective-permute-start | bytes 1572872 | tf_op jit(solution)/shard_map/ppermute | solution.py:64
  68.9 10.3 %collective-permute-done.2 = bf16[1024,256]{1,0:T(8,128)(2,1)} collective-permute-done((bf16[1024,256]{1,0:T(8,128)(2,1)}, bf16[1024,256]{1,0:T(8,128)(2,1)}, u32[]{:S(2)}, u32[]{:S(2)}) %collective-permute-start.2) | collective-permute-done | bytes 524320 | tf_op jit(solution)/shard_map/ppermute | solution.py:59
  81.0 3.6 %collective-permute-start.5 = (bf16[1024,256]{1,0:T(8,128)(2,1)}, bf16[1024,256]{1,0:T(8,128)(2,1)S(1)}, u32[]{:S(2)}, u32[]{:S(2)}) collective-permute-start(bf16[1024,256]{1,0:T(8,128)(2,1)} %collective-permute-done.3), channel_id=1, source_target_pairs={{0,7},{1,0},{2,1},{3,2},{4,3},{5,4},{6,5},{7,6},{8,15},{9,8},{10,9... | collective-permute-start | bytes 1572872 | tf_op jit(solution)/shard_map/ppermute | solution.py:64
  86.4 7.6 %collective-permute-done.4 = bf16[1024,256]{1,0:T(8,128)(2,1)S(1)} collective-permute-done((bf16[1024,256]{1,0:T(8,128)(2,1)}, bf16[1024,256]{1,0:T(8,128)(2,1)S(1)}, u32[]{:S(2)}, u32[]{:S(2)}) %collective-permute-start.4) | collective-permute-done | bytes 524320 | tf_op jit(solution)/shard_map/ppermute | solution.py:59
  97.8 1.9 constant_dynamic-update-slice_fusion.3
  101.4 3.1 %collective-permute-done.6 = bf16[1024,256]{1,0:T(8,128)(2,1)S(1)} collective-permute-done((bf16[1024,256]{1,0:T(8,128)(2,1)S(1)}, bf16[1024,256]{1,0:T(8,128)(2,1)S(1)}, u32[]{:S(2)}, u32[]{:S(2)}) %collective-permute-start.6) | collective-permute-done | bytes 524320 | tf_op jit(solution)/shard_map/ppermute | solution.py:59
  105.3 62.7 %while.14 = (s32[]{:T(128)}, f32[128,16,128]{2,0,1:T(8,128)S(1)}, f32[128,16]{0,1:T(8,128)S(1)}, f32[128,16]{0,1:T(8,128)S(1)}, s32[8]{0:T(128)S(1)}, /*index=5*...) while((s32[]{:T(128)}, f32[128,16,128]{2,0,1:T(8,128)S(1)}, ...), condition=%wide.region_10.11_spmd, body=%wide.region_7.10_spmd.sunk | while | flops 1091047424 | bytes 28442832 | solution.py:93
  106.5 2.2 bitcast_reduce_fusion.2
  110.1 2.9 %fusion.69 = f32[128,16,128]{2,0,1:T(8,128)S(1)} fusion(f32[1024,128,16]{1,0,2:T(8,128)S(1)} %get-tuple-element.137, f32[128,16]{0,1:T(8,128)S(1)} %max.4, f32[128,16,128]{2,0,1:T(8,128)S(1)} %get-tuple-element.154, f32[128,16]{0,1:T(8,128)S(1)} %get-tuple-element.139, bf16[8192,256]{1,0:T(8,128)(2,1)} %get-tuple-element.170, s32[]{:T(128)S(6)} %select_n.116, ...), kind=kOutput, calls=%fused_computation.8.clone.1 | convolution fusion | flops 543686656 | bytes 10764296 | tf_op jit(solution)/shard_map/while/body/eval_jaxpr/thp,pd->thd/dot_general | solution.py:85
  114.4 2.2 bitcast_reduce_fusion.2
  118.0 2.9 %fusion.69 = f32[128,16,128]{2,0,1:T(8,128)S(1)} fusion(f32[1024,128,16]{1,0,2:T(8,128)S(1)} %get-tuple-element.137, f32[128,16]{0,1:T(8,128)S(1)} %max.4, f32[128,16,128]{2,0,1:T(8,128)S(1)} %get-tuple-element.154, f32[128,16]{0,1:T(8,128)S(1)} %get-tuple-element.139, bf16[8192,256]{1,0:T(8,128)(2,1)} %get-tuple-element.170, s32[]{:T(128)S(6)} %select_n.116, ...), kind=kOutput, calls=%fused_computation.8.clone.1 | convolution fusion | flops 543686656 | bytes 10764296 | tf_op jit(solution)/shard_map/while/body/eval_jaxpr/thp,pd->thd/dot_general | solution.py:85
  122.2 2.2 bitcast_reduce_fusion.2
  125.8 2.9 %fusion.69 = f32[128,16,128]{2,0,1:T(8,128)S(1)} fusion(f32[1024,128,16]{1,0,2:T(8,128)S(1)} %get-tuple-element.137, f32[128,16]{0,1:T(8,128)S(1)} %max.4, f32[128,16,128]{2,0,1:T(8,128)S(1)} %get-tuple-element.154, f32[128,16]{0,1:T(8,128)S(1)} %get-tuple-element.139, bf16[8192,256]{1,0:T(8,128)(2,1)} %get-tuple-element.170, s32[]{:T(128)S(6)} %select_n.116, ...), kind=kOutput, calls=%fused_computation.8.clone.1 | convolution fusion | flops 543686656 | bytes 10764296 | tf_op jit(solution)/shard_map/while/body/eval_jaxpr/thp,pd->thd/dot_general | solution.py:85
  130.0 2.2 bitcast_reduce_fusion.2
  133.7 2.9 %fusion.69 = f32[128,16,128]{2,0,1:T(8,128)S(1)} fusion(f32[1024,128,16]{1,0,2:T(8,128)S(1)} %get-tuple-element.137, f32[128,16]{0,1:T(8,128)S(1)} %max.4, f32[128,16,128]{2,0,1:T(8,128)S(1)} %get-tuple-element.154, f32[128,16]{0,1:T(8,128)S(1)} %get-tuple-element.139, bf16[8192,256]{1,0:T(8,128)(2,1)} %get-tuple-element.170, s32[]{:T(128)S(6)} %select_n.116, ...), kind=kOutput, calls=%fused_computation.8.clone.1 | convolution fusion | flops 543686656 | bytes 10764296 | tf_op jit(solution)/shard_map/while/body/eval_jaxpr/thp,pd->thd/dot_general | solution.py:85
  137.9 2.2 bitcast_reduce_fusion.2
  141.5 2.9 %fusion.69 = f32[128,16,128]{2,0,1:T(8,128)S(1)} fusion(f32[1024,128,16]{1,0,2:T(8,128)S(1)} %get-tuple-element.137, f32[128,16]{0,1:T(8,128)S(1)} %max.4, f32[128,16,128]{2,0,1:T(8,128)S(1)} %get-tuple-element.154, f32[128,16]{0,1:T(8,128)S(1)} %get-tuple-element.139, bf16[8192,256]{1,0:T(8,128)(2,1)} %get-tuple-element.170, s32[]{:T(128)S(6)} %select_n.116, ...), kind=kOutput, calls=%fused_computation.8.clone.1 | convolution fusion | flops 543686656 | bytes 10764296 | tf_op jit(solution)/shard_map/while/body/eval_jaxpr/thp,pd->thd/dot_general | solution.py:85
  145.7 2.2 bitcast_reduce_fusion.2
  149.3 2.9 %fusion.69 = f32[128,16,128]{2,0,1:T(8,128)S(1)} fusion(f32[1024,128,16]{1,0,2:T(8,128)S(1)} %get-tuple-element.137, f32[128,16]{0,1:T(8,128)S(1)} %max.4, f32[128,16,128]{2,0,1:T(8,128)S(1)} %get-tuple-element.154, f32[128,16]{0,1:T(8,128)S(1)} %get-tuple-element.139, bf16[8192,256]{1,0:T(8,128)(2,1)} %get-tuple-element.170, s32[]{:T(128)S(6)} %select_n.116, ...), kind=kOutput, calls=%fused_computation.8.clone.1 | convolution fusion | flops 543686656 | bytes 10764296 | tf_op jit(solution)/shard_map/while/body/eval_jaxpr/thp,pd->thd/dot_general | solution.py:85
  153.6 2.2 bitcast_reduce_fusion.2
  157.2 2.9 %fusion.69 = f32[128,16,128]{2,0,1:T(8,128)S(1)} fusion(f32[1024,128,16]{1,0,2:T(8,128)S(1)} %get-tuple-element.137, f32[128,16]{0,1:T(8,128)S(1)} %max.4, f32[128,16,128]{2,0,1:T(8,128)S(1)} %get-tuple-element.154, f32[128,16]{0,1:T(8,128)S(1)} %get-tuple-element.139, bf16[8192,256]{1,0:T(8,128)(2,1)} %get-tuple-element.170, s32[]{:T(128)S(6)} %select_n.116, ...), kind=kOutput, calls=%fused_computation.8.clone.1 | convolution fusion | flops 543686656 | bytes 10764296 | tf_op jit(solution)/shard_map/while/body/eval_jaxpr/thp,pd->thd/dot_general | solution.py:85
  161.4 2.2 bitcast_reduce_fusion.2
  165.0 2.9 %fusion.69 = f32[128,16,128]{2,0,1:T(8,128)S(1)} fusion(f32[1024,128,16]{1,0,2:T(8,128)S(1)} %get-tuple-element.137, f32[128,16]{0,1:T(8,128)S(1)} %max.4, f32[128,16,128]{2,0,1:T(8,128)S(1)} %get-tuple-element.154, f32[128,16]{0,1:T(8,128)S(1)} %get-tuple-element.139, bf16[8192,256]{1,0:T(8,128)(2,1)} %get-tuple-element.170, s32[]{:T(128)S(6)} %select_n.116, ...), kind=kOutput, calls=%fused_computation.8.clone.1 | convolution fusion | flops 543686656 | bytes 10764296 | tf_op jit(solution)/shard_map/while/body/eval_jaxpr/thp,pd->thd/dot_general | solution.py:85
  170.7 4.8 %fusion.51 = (f32[128]{0:T(128)S(1)}, f32[128,2048]{1,0:T(8,128)S(1)}) fusion(bf16[128,2048]{0,1:T(8,128)(2,1)S(1)} %bitcast.90, bf16[2048,2048]{1,0:T(8,128)(2,1)} %param.25, bf16[1,128,2048]{2,1,0:T(8,128)(2,1)S(1)} %copy-done.2), kind=kOutput, calls=%fused_computation.84 | convolution fusion | flops 1074528128 | bytes 10486272 | tf_op jit(solution)/shard_map/dot_general | solution.py:137
  177.1 44.3 %all-gather.5.cloned.1.call-done = bf16[1024,2048]{1,0:T(8,128)(2,1)} async-done(((bf16[128,2048]{1,0:T(8,128)(2,1)}), bf16[1024,2048]{1,0:T(8,128)(2,1)}) %all-gather.5.cloned.1.call-update) | async-done | bytes 4194320 | tf_op jit(solution)/shard_map/all_gather | solution.py:141
  221.4 15.1 %convolution_convert_fusion = bf16[1024,2048]{1,0:T(8,128)(2,1)} fusion(bf16[1024,2048]{1,0:T(8,128)(2,1)} %param.29, bf16[1024,2048]{1,0:T(8,128)(2,1)} %all-gather.5.cloned.1.call-done, bf16[2048,1024]{1,0:T(8,128)(2,1)} %param.28), kind=kOutput, calls=%fused_computation.25 | convolution fusion | flops 8601468928 | bytes 16777216 | tf_op jit(solution)/shard_map/dot_general | solution.py:148
  239.6 45.8 %reduce-scatter.2.cloned.1.call-done = bf16[128,2048]{1,0:T(8,128)(2,1)} async-done(((bf16[1024,2048]{1,0:T(8,128)(2,1)}), bf16[128,2048]{1,0:T(8,128)(2,1)}) %reduce-scatter.2.cloned.1.call-update) | async-done | bytes 524304 | tf_op jit(solution)/shard_map/reduce_scatter | solution.py:147
  285.4 2.0 fusion.39
  (104 shorter events, 41.2 us)
Async XLA Ops:
  6.5 56.4 %copy-start = (bf16[2048,256]{1,0:T(8,128)(2,1)S(1)}, bf16[2048,256]{1,0:T(8,128)(2,1)}, u32[]{:S(2)}) copy-start(bf16[2048,256]{1,0:T(8,128)(2,1)} %param.24) | copy-start | bytes 3145732
  6.5 45.7 %copy-start.2 = (bf16[1,128,2048]{2,1,0:T(8,128)(2,1)S(1)}, bf16[1,128,2048]{2,1,0:T(8,128)(2,1)}, u32[]{:S(2)}) copy-start(bf16[1,128,2048]{2,1,0:T(8,128)(2,1)} %param.16) | copy-start | bytes 1572868
  6.5 45.7 %copy-start.7 = (f32[2048]{0:T(1024)S(1)}, f32[2048]{0:T(1024)}, u32[]{:S(2)}) copy-start(f32[2048]{0:T(1024)} %param.22) | copy-start | bytes 24580
  6.5 45.7 %copy-start.8 = (f32[2048]{0:T(1024)S(1)}, f32[2048]{0:T(1024)}, u32[]{:S(2)}) copy-start(f32[2048]{0:T(1024)} %param.21) | copy-start | bytes 24580
  6.5 40.7 %all-gather.3.cloned.1.call-start = ((), (), s32[]{:S(2)}) async-start(), calls=%async_computation.1 | async-start | bytes 2621440 | tf_op jit(solution)/shard_map/all_gather | solution.py:127
  7.3 214.1 %all-gather.5.cloned.1.call-start = ((), (), s32[]{:S(2)}) async-start(), calls=%async_computation.2 | async-start | bytes 4718592 | tf_op jit(solution)/shard_map/all_gather | solution.py:141
  48.7 8.3 %copy-start.1 = (bf16[8192,256]{1,0:T(8,128)(2,1)}, bf16[8192,256]{1,0:T(8,128)(2,1)S(1)}, u32[]{:S(2)}) copy-start(bf16[8192,256]{1,0:T(8,128)(2,1)S(1)} %get-tuple-element.82) | copy-start | bytes 12582916
  48.7 14.3 %collective-permute-start = (bf16[1024,256]{1,0:T(8,128)(2,1)S(1)}, bf16[1024,256]{1,0:T(8,128)(2,1)}, u32[]{:S(2)}, u32[]{:S(2)}) collective-permute-start(bf16[1024,256]{1,0:T(8,128)(2,1)S(1)} %get-tuple-element.83), channel_id=1, source_target_pairs={{0,1},{1,2},{2,3},{3,4},{4,5},{5,6},{6,7},{7,0},{8,9},{9,10},{10,1... | collective-permute-start | bytes 1572872 | tf_op jit(solution)/shard_map/ppermute | solution.py:59
  48.7 14.6 %collective-permute-start.1 = (bf16[1024,256]{1,0:T(8,128)(2,1)S(1)}, bf16[1024,256]{1,0:T(8,128)(2,1)}, u32[]{:S(2)}, u32[]{:S(2)}) collective-permute-start(bf16[1024,256]{1,0:T(8,128)(2,1)S(1)} %get-tuple-element.83), channel_id=1, source_target_pairs={{0,7},{1,0},{2,1},{3,2},{4,3},{5,4},{6,5},{7,6},{8,15},{9,8},{10,9... | collective-permute-start | bytes 1572872 | tf_op jit(solution)/shard_map/ppermute | solution.py:64
  57.0 10.4 %copy-start.4 = (bf16[16,16,8,128]{3,2,1,0:T(8,128)(2,1)}, bf16[16,16,8,128]{3,2,1,0:T(8,128)(2,1)S(1)}, u32[]{:S(2)}) copy-start(bf16[16,16,8,128]{3,2,1,0:T(8,128)(2,1)S(1)} %fusion.30) | copy-start | bytes 1572868
  63.0 16.2 %collective-permute-start.2 = (bf16[1024,256]{1,0:T(8,128)(2,1)}, bf16[1024,256]{1,0:T(8,128)(2,1)}, u32[]{:S(2)}, u32[]{:S(2)}) collective-permute-start(bf16[1024,256]{1,0:T(8,128)(2,1)} %collective-permute-done), channel_id=1, source_target_pairs={{0,1},{1,2},{2,3},{3,4},{4,5},{5,6},{6,7},{7,0},{8,9},{9,10},{10,1... | collective-permute-start | bytes 1572872 | tf_op jit(solution)/shard_map/ppermute | solution.py:59
  63.4 17.6 %collective-permute-start.3 = (bf16[1024,256]{1,0:T(8,128)(2,1)}, bf16[1024,256]{1,0:T(8,128)(2,1)}, u32[]{:S(2)}, u32[]{:S(2)}) collective-permute-start(bf16[1024,256]{1,0:T(8,128)(2,1)} %collective-permute-done.1), channel_id=1, source_target_pairs={{0,7},{1,0},{2,1},{3,2},{4,3},{5,4},{6,5},{7,6},{8,15},{9,8},{10,9... | collective-permute-start | bytes 1572872 | tf_op jit(solution)/shard_map/ppermute | solution.py:64
  67.3 11.9 %copy-start.3 = (f32[128,16,128]{0,2,1:T(8,128)}, f32[128,16,128]{0,2,1:T(8,128)S(1)}, u32[]{:S(2)}) copy-start(f32[128,16,128]{0,2,1:T(8,128)S(1)} %get-tuple-element.87) | copy-start | bytes 3145732
  79.2 14.8 %collective-permute-start.4 = (bf16[1024,256]{1,0:T(8,128)(2,1)}, bf16[1024,256]{1,0:T(8,128)(2,1)S(1)}, u32[]{:S(2)}, u32[]{:S(2)}) collective-permute-start(bf16[1024,256]{1,0:T(8,128)(2,1)} %collective-permute-done.2), channel_id=1, source_target_pairs={{0,1},{1,2},{2,3},{3,4},{4,5},{5,6},{6,7},{7,0},{8,9},{9,10},{10,1... | collective-permute-start | bytes 1572872 | tf_op jit(solution)/shard_map/ppermute | solution.py:59
  81.0 19.6 %collective-permute-start.5 = (bf16[1024,256]{1,0:T(8,128)(2,1)}, bf16[1024,256]{1,0:T(8,128)(2,1)S(1)}, u32[]{:S(2)}, u32[]{:S(2)}) collective-permute-start(bf16[1024,256]{1,0:T(8,128)(2,1)} %collective-permute-done.3), channel_id=1, source_target_pairs={{0,7},{1,0},{2,1},{3,2},{4,3},{5,4},{6,5},{7,6},{8,15},{9,8},{10,9... | collective-permute-start | bytes 1572872 | tf_op jit(solution)/shard_map/ppermute | solution.py:64
  94.0 10.4 %collective-permute-start.6 = (bf16[1024,256]{1,0:T(8,128)(2,1)S(1)}, bf16[1024,256]{1,0:T(8,128)(2,1)S(1)}, u32[]{:S(2)}, u32[]{:S(2)}) collective-permute-start(bf16[1024,256]{1,0:T(8,128)(2,1)S(1)} %collective-permute-done.4), channel_id=1, source_target_pairs={{0,1},{1,2},{2,3},{3,4},{4,5},{5,6},{6,7},{7,0},{8,9},{9,10},{10,1... | collective-permute-start | bytes 1572872 | tf_op jit(solution)/shard_map/ppermute | solution.py:59
  170.7 5.1 %copy-start.5 = (f32[2048]{0:T(1024)S(1)}, f32[2048]{0:T(1024)}, u32[]{:S(2)}) copy-start(f32[2048]{0:T(1024)} %param.27) | copy-start | bytes 24580
  170.7 5.1 %copy-start.6 = (f32[2048]{0:T(1024)S(1)}, f32[2048]{0:T(1024)}, u32[]{:S(2)}) copy-start(f32[2048]{0:T(1024)} %param.26) | copy-start | bytes 24580
  176.8 108.6 %reduce-scatter.2.cloned.1.call-start = ((), (), s32[]{:S(2)}) async-start(), calls=%async_computation.3 | async-start | bytes 4718592 | tf_op jit(solution)/shard_map/reduce_scatter | solution.py:147
  236.5 0.7 copy-start.9
  236.5 1.3 copy-start.10
Sparse Core Ops, SparseCore 0:
  9.2 38.0 all-gather.2
  176.9 44.4 all-gather.4
  236.7 48.7 reduce-scatter.1
